TPU v7x, 256 devices: a whole 4x4x8 slice. The times are simulated.
256 devices in a mesh: section: 32 (over x, z), expert: 8 (over y, core).
Axes of the slice: x: 4, y: 4, z: 8, core: 2. Of those that a mesh axis runs over, the one named last changes fastest.
Arguments:
- tokens: bfloat16 [2048, 4096], P('expert', 'section'), may hold values from -6 to 6
- routes: int32 [2048, 2], P('expert'), may hold values from 0 to 7, all different within a row; in each aligned block of 256 rows (0 to 255, 256 to 511, ...) at most 80 rows name the same one
- mix_weights: float32 [2048, 2], P('expert'), may hold values from 0.2 to 1
- w_gate: bfloat16 [8, 4096, 8192], P('expert', None, 'section'), may hold values from -0.1875 to 0.1875
- w_up: bfloat16 [8, 4096, 8192], P('expert', None, 'section'), may hold values from -0.1875 to 0.1875
- w_down: bfloat16 [8, 8192, 4096], P('expert', 'section'), may hold values from -0.125 to 0.125
- upstream: bfloat16 [2048, 4096], P('expert', 'section'), may hold values from -6 to 6
Outputs:
- mixed: bfloat16 [2048, 4096], P('expert', 'section')
- grad_tokens: bfloat16 [2048, 4096], P('expert', 'section')
- grad_mix: float32 [2048, 2], P('expert')
- grad_gate: bfloat16 [8, 4096, 8192], P('expert', None, 'section')
- grad_up: bfloat16 [8, 4096, 8192], P('expert', None, 'section')
- grad_down: bfloat16 [8, 8192, 4096], P('expert', 'section')
Inputs may be any that keep to these rules, and one draw needn't show every extreme that they name: `routes`: each token names 2 different experts. Among the 256 tokens of one index of the expert axis no expert is named more than 80 times, and in some such block one expert is named exactly 80 times.
All inputs are finite; a program needn't handle non-finite values.
Results may differ from a plain program's by a relative error of at most 0.02.
Values may be sent and summed in bfloat16 or wider, within the bound.
No kernel may reach another device: no remote copies, remote signals or barrier semaphores. Data moves between devices by JAX's collectives and lax.ppermute only.
A program may use at most 128 MiB of HBM per device.

v0:
```python
import jax
import jax.numpy as jnp
from jax import lax
from jax.sharding import PartitionSpec as P

highest = lax.Precision.HIGHEST


def slot_tables(route_rows, mix_rows, capacity, experts):
    tok_count, top_count = route_rows.shape
    flat_routes = route_rows.reshape(-1)
    onehot = (flat_routes[:, None] == jnp.arange(experts, dtype=jnp.int32)[None, :]).astype(
        jnp.int32
    )
    earlier = jnp.cumsum(onehot, axis=0) - onehot
    position = jnp.sum(earlier * onehot, axis=1)
    target = (flat_routes * capacity + position).reshape(tok_count, top_count)
    slot_ids = jnp.arange(experts * capacity, dtype=jnp.int32)
    hits = target[None, :, :] == slot_ids[:, None, None]
    matches = hits.astype(jnp.float32)
    select = jnp.sum(matches, axis=2)
    weighted = jnp.sum(matches * mix_rows[None, :, :], axis=2)
    token_ids = jnp.arange(tok_count, dtype=jnp.int32)
    slot_token = jnp.sum(jnp.sum(hits.astype(jnp.int32), axis=2) * token_ids[None, :], axis=1)
    return (target, select, weighted, slot_token)


def per_device(tokens, routes, mix_weights, w_gate, w_up, w_down, upstream):
    experts = lax.axis_size("expert")
    tok_count = tokens.shape[0]
    top_count = routes.shape[1]
    capacity = 5 * tok_count * top_count // (4 * experts)
    slot_total = experts * capacity
    target, select, weighted, slot_token = slot_tables(routes, mix_weights, capacity, experts)
    slot_fill = jnp.sum(select, axis=1)
    slot_scale = jnp.sum(weighted, axis=1)
    gate_local = w_gate[0]
    up_local = w_up[0]
    down_local = w_down[0]

    def collect(source, factor):
        taken = source[slot_token].astype(jnp.float32)
        return (taken * factor[:, None]).astype(jnp.bfloat16)

    def to_experts(source, factor):
        block = collect(source, factor)
        arrived = lax.all_to_all(
            block.reshape(experts, capacity, -1), "expert", split_axis=0, concat_axis=0, tiled=True
        )
        whole = lax.all_gather(arrived, "section", axis=2, tiled=True)
        return whole.reshape(slot_total, -1)

    def to_sources(partial_value):
        summed = lax.psum_scatter(
            partial_value.reshape(experts, capacity, -1).astype(jnp.bfloat16),
            "section",
            scatter_dimension=2,
            tiled=True,
        )
        back = lax.all_to_all(summed, "expert", split_axis=0, concat_axis=0, tiled=True)
        return back.reshape(slot_total, -1)

    dispatched = to_experts(tokens, slot_fill)
    act_gate = jnp.dot(dispatched, gate_local, preferred_element_type=jnp.float32)
    act_up = jnp.dot(dispatched, up_local, preferred_element_type=jnp.float32)
    sig = jax.nn.sigmoid(act_gate)
    silu_gate = act_gate * sig
    hidden = (silu_gate * act_up).astype(jnp.bfloat16)
    partial_value = jnp.dot(hidden, down_local, preferred_element_type=jnp.float32)
    returned = to_sources(partial_value).astype(jnp.float32)
    moe_out = jnp.dot(weighted.T, returned, precision=highest)
    mixed = (tokens.astype(jnp.float32) + moe_out).astype(jnp.bfloat16)
    picked = returned[target]
    upstream_wide = upstream.astype(jnp.float32)
    mix_terms = jnp.einsum("tkd,td->tk", picked, upstream_wide, precision=highest)
    grad_mix = lax.psum(mix_terms, "section")
    grad_rows = to_experts(upstream, slot_scale)
    grad_hidden = lax.dot_general(
        grad_rows, down_local, (((1,), (1,)), ((), ())), preferred_element_type=jnp.float32
    )
    grad_down = lax.dot_general(
        hidden, grad_rows, (((0,), (0,)), ((), ())), preferred_element_type=jnp.float32
    ).astype(jnp.bfloat16)
    dsilu = sig * (1.0 + act_gate * (1.0 - sig))
    grad_act_gate = (grad_hidden * act_up * dsilu).astype(jnp.bfloat16)
    grad_act_up = (grad_hidden * silu_gate).astype(jnp.bfloat16)
    grad_gate = lax.dot_general(
        dispatched, grad_act_gate, (((0,), (0,)), ((), ())), preferred_element_type=jnp.float32
    ).astype(jnp.bfloat16)
    grad_up = lax.dot_general(
        dispatched, grad_act_up, (((0,), (0,)), ((), ())), preferred_element_type=jnp.float32
    ).astype(jnp.bfloat16)
    first = lax.dot_general(
        grad_act_gate, gate_local, (((1,), (1,)), ((), ())), preferred_element_type=jnp.float32
    )
    second = lax.dot_general(
        grad_act_up, up_local, (((1,), (1,)), ((), ())), preferred_element_type=jnp.float32
    )
    back_rows = to_sources(first + second).astype(jnp.float32)
    grad_moe = jnp.dot(select.T, back_rows, precision=highest)
    grad_tokens = (upstream_wide + grad_moe).astype(jnp.bfloat16)
    return (mixed, grad_tokens, grad_mix, grad_gate[None], grad_up[None], grad_down[None])


def solution(mesh):
    return jax.shard_map(
        per_device,
        mesh=mesh,
        in_specs=(
            P("expert", "section"),
            P("expert", None),
            P("expert", None),
            P("expert", None, "section"),
            P("expert", None, "section"),
            P("expert", "section", None),
            P("expert", "section"),
        ),
        out_specs=(
            P("expert", "section"),
            P("expert", "section"),
            P("expert", None),
            P("expert", None, "section"),
            P("expert", None, "section"),
            P("expert", "section", None),
        ),
        check_vma=False,
    )
```

profile of v0, /device:TPU:8, one launch (start us, length us, event | category | flops | bytes accessed | tf_op | source)
XLA Modules:
  0.0 783.5 jit_solution(15971595313948356913)
XLA Ops:
  8.5 1.1 reduce-window.6
  11.4 2.1 select_reduce_fusion
  13.6 2.0 gather_fusion
  15.7 10.3 %all_to_all.20 = bf16[8,80,128]{2,1,0:T(8,128)(2,1)} all-to-all(bf16[8,80,128]{2,1,0:T(8,128)(2,1)S(1)} %fusion.17), channel_id=1, replica_groups=mesh['section'=32,'expert'=8] {'expert'}, dimensions={0} | all-to-all | bytes 327680 | tf_op jit(solution)/shard_map/all_to_all | solution.py:47
  26.1 2.0 gather_fusion.1
  28.3 9.5 %all_to_all.21 = bf16[8,80,128]{2,1,0:T(8,128)(2,1)} all-to-all(bf16[8,80,128]{2,1,0:T(8,128)(2,1)S(1)} %fusion.16), channel_id=1, replica_groups=mesh['section'=32,'expert'=8] {'expert'}, dimensions={0} | all-to-all | bytes 327680 | tf_op jit(solution)/shard_map/all_to_all | solution.py:47
  37.9 77.2 %all-gather.3.cloned.1.call-done = bf16[8,80,4096]{2,1,0:T(8,128)(2,1)} async-done(((bf16[8,80,128]{2,1,0:T(8,128)(2,1)}), bf16[8,80,4096]{2,1,0:T(8,128)(2,1)}) %all-gather.3.cloned.1.call-update) | async-done | bytes 5242896 | tf_op jit(solution)/shard_map/all_gather | solution.py:50
  115.2 5.7 fusion.7
  120.8 2.4 fusion.11
  123.2 81.6 %all-gather.5.cloned.1.call-done = bf16[8,80,4096]{2,1,0:T(8,128)(2,1)} async-done(((bf16[8,80,128]{2,1,0:T(8,128)(2,1)}), bf16[8,80,4096]{2,1,0:T(8,128)(2,1)}) %all-gather.5.cloned.1.call-update) | async-done | bytes 5242896 | tf_op jit(solution)/shard_map/all_gather | solution.py:50
  204.7 5.4 multiply_convert_fusion
  210.1 3.9 convolution_convert_fusion
  214.0 11.2 %copy.36 = bf16[8,80,4096]{1,0,2:T(8,128)(2,1)} copy(bf16[8,80,4096]{2,1,0:T(8,128)(2,1)} %convolution_convert_fusion) | data formatting | bytes 10485760
  225.2 13.1 %reshape.124 = bf16[4096,640]{1,0:T(8,128)(2,1)} reshape(bf16[4096,8,80]{2,1,0:T(8,128)(2,1)} %bitcast.66) | data formatting | bytes 10485760
  238.5 1.3 copy-done.5
  239.8 2.7 fusion.9
  242.5 3.9 add_convert_fusion
  246.4 11.2 %copy.38 = bf16[8,80,4096]{1,0,2:T(8,128)(2,1)} copy(bf16[8,80,4096]{2,1,0:T(8,128)(2,1)} %bitcast.69) | data formatting | bytes 10485760
  257.6 13.1 %reshape.126 = bf16[4096,640]{1,0:T(8,128)(2,1)} reshape(bf16[4096,8,80]{2,1,0:T(8,128)(2,1)} %bitcast.67) | data formatting | bytes 10485760
  271.7 5.7 fusion.1
  277.4 5.8 fusion
  283.2 180.6 %reduce-scatter.7.cloned.1.call-done = bf16[128,640]{1,0:T(8,128)(2,1)} async-done(((bf16[4096,640]{1,0:T(8,128)(2,1)}), bf16[128,640]{1,0:T(8,128)(2,1)}) %reduce-scatter.7.cloned.1.call-update) | async-done | bytes 163856
  463.8 1.2 reshape.125
  465.8 4.8 all-to-all-start.1
  470.6 5.8 fusion.2
  476.4 215.3 %reduce-scatter.9.cloned.1.call-done = bf16[128,640]{1,0:T(8,128)(2,1)} async-done(((bf16[4096,640]{1,0:T(8,128)(2,1)}), bf16[128,640]{1,0:T(8,128)(2,1)}) %reduce-scatter.9.cloned.1.call-update) | async-done | bytes 163856
  691.7 1.2 reshape.127
  693.7 4.8 all-to-all-start.3
  698.5 1.3 gather_fusion.2
  700.3 72.8 %psum.7 = f32[256,2]{0,1:T(2,128)} all-reduce(f32[256,2]{0,1:T(2,128)S(1)} %bitcast.81), channel_id=1, replica_groups=mesh['section'=32,'expert'=8] {'section'}, use_global_device_ids=true, to_apply=%region_11.12 | all-reduce | flops 512 | bytes 4096 | tf_op jit(solution)/shard_map/psum | solution.py:76
  773.2 2.4 fusion.13
  775.6 1.4 fusion.14
  (57 shorter events, 7.0 us)
Async XLA Ops:
  7.2 197.6 %copy-start = (bf16[1,256,4096]{2,1,0:T(8,128)(2,1)S(1)}, bf16[1,256,4096]{2,1,0:T(8,128)(2,1)}, u32[]{:S(2)}) copy-start(bf16[1,256,4096]{2,1,0:T(8,128)(2,1)} %param.12) | copy-start | bytes 6291460
  7.2 6.4 copy-start.2
  7.2 18.9 %copy-start.3 = (bf16[256,128]{1,0:T(8,128)(2,1)S(1)}, bf16[256,128]{1,0:T(8,128)(2,1)}, u32[]{:S(2)}) copy-start(bf16[256,128]{1,0:T(8,128)(2,1)} %param.13) | copy-start | bytes 196612
  7.2 108.0 %all-gather.3.cloned.1.call-start = ((), (), s32[]{:S(2)}) async-start(), calls=%async_computation.6 | async-start | bytes 5406720 | tf_op jit(solution)/shard_map/all_gather | solution.py:50
  26.0 178.7 %all-gather.5.cloned.1.call-start = ((), (), s32[]{:S(2)}) async-start(), calls=%async_computation.7 | async-start | bytes 5406720 | tf_op jit(solution)/shard_map/all_gather | solution.py:50
  37.9 425.9 %reduce-scatter.7.cloned.1.call-start = ((), (), s32[]{:S(2)}) async-start(), calls=%async_computation.8 | async-start | bytes 5406720
  115.2 5.7 copy-start.4
  115.2 5.7 copy-start.10
  238.2 1.6 copy-start.5
  238.3 453.4 %reduce-scatter.9.cloned.1.call-start = ((), (), s32[]{:S(2)}) async-start(), calls=%async_computation.9 | async-start | bytes 5406720
  239.8 2.7 copy-start.6
  239.8 2.7 copy-start.8
  270.7 1.0 copy-start.9
  271.7 5.7 copy-start.7
  465.8 227.9 %all-to-all-start.1 = ((bf16[8,80,128]{2,1,0:T(8,128)(2,1)}), bf16[8,80,128]{2,1,0:T(8,128)(2,1)S(1)}, u32[]{:S(2)}, u32[]{:S(2)}) async-start(bf16[8,80,128]{2,1,0:T(8,128)(2,1)} %copy.37), calls=%async_computation.1 | async-start | bytes 327680 | tf_op jit(solution)/shard_map/all_to_all | solution.py:60
  470.6 306.3 %copy-start.1 = (bf16[1,256,4096]{2,1,0:T(8,128)(2,1)S(1)}, bf16[1,256,4096]{2,1,0:T(8,128)(2,1)}, u32[]{:S(2)}) copy-start(bf16[1,256,4096]{2,1,0:T(8,128)(2,1)} %param.12) | copy-start | bytes 6291460
  693.7 81.9 %all-to-all-start.3 = ((bf16[8,80,128]{2,1,0:T(8,128)(2,1)}), bf16[8,80,128]{2,1,0:T(8,128)(2,1)S(1)}, u32[]{:S(2)}, u32[]{:S(2)}) async-start(bf16[8,80,128]{2,1,0:T(8,128)(2,1)} %copy.39), calls=%async_computation.3 | async-start | bytes 327680 | tf_op jit(solution)/shard_map/all_to_all | solution.py:60
Sparse Core Ops, SparseCore 0:
  26.1 88.9 all-gather.2
  117.6 87.0 all-gather.4
  238.4 225.3 reduce-scatter.6
  467.6 224.0 reduce-scatter.8
where the time goes:
time: 785 us; the launch traced here: 783 us
  waiting for transfers between devices  555 us (71%)
  blocking collectives  92.6 us (12%)
  local copies, waits for them, and re-layouts  62.1 us (8%)
  matrix products  45.3 us (6%)
  between operations  14 us (2%)
  starting transfers between devices  9.93 us (1%)
    unnamed x6, waiting for transfers between devices  396 us
    all_gather x2, waiting for transfers between devices, to_experts(): whole = lax.all_gather(arrived, 'section', axis=2, tiled=True)  159 us
    psum x1, blocking collectives, per_device(): grad_mix = lax.psum(mix_terms, 'section')  72.8 us
    unnamed x31, local copies, waits for them, and re-layouts  55.6 us
    all_to_all x2, blocking collectives, to_experts(): lax.all_to_all(block.reshape(experts, capacity, -1), 'expert', split_axis...  19.8 us
  transfers between devices with their start and end apart: 6, of which 4 were waited for; matrix products, arithmetic and copies ran while one was open for 9% of the time, Pallas kernels for 0%

commit v1 on v0

--- a/solution.py
+++ b/solution.py
@@ -73,7 +73,8 @@
     picked = returned[target]
     upstream_wide = upstream.astype(jnp.float32)
     mix_terms = jnp.einsum("tkd,td->tk", picked, upstream_wide, precision=highest)
-    grad_mix = lax.psum(mix_terms, "section")
+    blocks = lax.all_gather(mix_terms, "section", axis=0, tiled=False)
+    grad_mix = blocks.sum(axis=0)
     grad_rows = to_experts(upstream, slot_scale)
     grad_hidden = lax.dot_general(
         grad_rows, down_local, (((1,), (1,)), ((), ())), preferred_element_type=jnp.float32

time: 785 us -> 760 us (0.968)
  blocking collectives: 92.6 us -> 67.1 us
    psum x1 -> x0, blocking collectives: 72.8 us -> none  [per_device(): grad_mix = lax.psum(mix_terms, 'section')]
    all_gather x0 -> x1, blocking collectives: none -> 47.3 us  [per_device(): blocks = lax.all_gather(mix_terms, 'section', axis=0, tiled=False)]
where the time goes in v1:
time: 760 us; the launch traced here: 759 us
  waiting for transfers between devices  555 us (73%)
  blocking collectives  67.1 us (9%)
  local copies, waits for them, and re-layouts  62.1 us (8%)
  matrix products  45.3 us (6%)
  between operations  14 us (2%)
  starting transfers between devices  9.93 us (1%)
    unnamed x6, waiting for transfers between devices  396 us
    all_gather x2, waiting for transfers between devices, to_experts(): whole = lax.all_gather(arrived, 'section', axis=2, tiled=True)  159 us
    unnamed x31, local copies, waits for them, and re-layouts  55.6 us
    all_gather x1, blocking collectives, per_device(): blocks = lax.all_gather(mix_terms, 'section', axis=0, tiled=False)  47.3 us
    all_to_all x2, blocking collectives, to_experts(): lax.all_to_all(block.reshape(experts, capacity, -1), 'expert', split_axis...  19.8 us
  transfers between devices with their start and end apart: 6, of which 4 were waited for; matrix products, arithmetic and copies ran while one was open for 9% of the time, Pallas kernels for 0%

profile of v1, /device:TPU:8, one launch (start us, length us, event | category | flops | bytes accessed | tf_op | source)
XLA Modules:
  0.0 758.6 jit_solution(1219701006965071149)
XLA Ops:
  8.5 1.1 reduce-window.6
  11.4 2.1 select_reduce_fusion
  13.6 2.0 gather_fusion
  15.7 10.3 %all_to_all.20 = bf16[8,80,128]{2,1,0:T(8,128)(2,1)} all-to-all(bf16[8,80,128]{2,1,0:T(8,128)(2,1)S(1)} %fusion.17), channel_id=1, replica_groups=mesh['section'=32,'expert'=8] {'expert'}, dimensions={0} | all-to-all | bytes 327680 | tf_op jit(solution)/shard_map/all_to_all | solution.py:47
  26.1 2.0 gather_fusion.1
  28.3 9.5 %all_to_all.21 = bf16[8,80,128]{2,1,0:T(8,128)(2,1)} all-to-all(bf16[8,80,128]{2,1,0:T(8,128)(2,1)S(1)} %fusion.16), channel_id=1, replica_groups=mesh['section'=32,'expert'=8] {'expert'}, dimensions={0} | all-to-all | bytes 327680 | tf_op jit(solution)/shard_map/all_to_all | solution.py:47
  37.9 77.2 %all-gather.4.cloned.1.call-done = bf16[8,80,4096]{2,1,0:T(8,128)(2,1)} async-done(((bf16[8,80,128]{2,1,0:T(8,128)(2,1)}), bf16[8,80,4096]{2,1,0:T(8,128)(2,1)}) %all-gather.4.cloned.1.call-update) | async-done | bytes 5242896 | tf_op jit(solution)/shard_map/all_gather | solution.py:50
  115.2 5.7 fusion.7
  120.8 2.4 fusion.11
  123.2 81.6 %all-gather.6.cloned.1.call-done = bf16[8,80,4096]{2,1,0:T(8,128)(2,1)} async-done(((bf16[8,80,128]{2,1,0:T(8,128)(2,1)}), bf16[8,80,4096]{2,1,0:T(8,128)(2,1)}) %all-gather.6.cloned.1.call-update) | async-done | bytes 5242896 | tf_op jit(solution)/shard_map/all_gather | solution.py:50
  204.7 5.4 multiply_convert_fusion
  210.1 3.9 convolution_convert_fusion
  214.0 11.2 %copy.36 = bf16[8,80,4096]{1,0,2:T(8,128)(2,1)} copy(bf16[8,80,4096]{2,1,0:T(8,128)(2,1)} %convolution_convert_fusion) | data formatting | bytes 10485760
  225.2 13.1 %reshape.125 = bf16[4096,640]{1,0:T(8,128)(2,1)} reshape(bf16[4096,8,80]{2,1,0:T(8,128)(2,1)} %bitcast.71) | data formatting | bytes 10485760
  238.5 1.3 copy-done.5
  239.8 2.7 fusion.9
  242.5 3.9 add_convert_fusion
  246.4 11.2 %copy.38 = bf16[8,80,4096]{1,0,2:T(8,128)(2,1)} copy(bf16[8,80,4096]{2,1,0:T(8,128)(2,1)} %bitcast.74) | data formatting | bytes 10485760
  257.6 13.1 %reshape.127 = bf16[4096,640]{1,0:T(8,128)(2,1)} reshape(bf16[4096,8,80]{2,1,0:T(8,128)(2,1)} %bitcast.72) | data formatting | bytes 10485760
  271.7 5.7 fusion.1
  277.4 5.8 fusion
  283.2 180.6 %reduce-scatter.7.cloned.1.call-done = bf16[128,640]{1,0:T(8,128)(2,1)} async-done(((bf16[4096,640]{1,0:T(8,128)(2,1)}), bf16[128,640]{1,0:T(8,128)(2,1)}) %reduce-scatter.7.cloned.1.call-update) | async-done | bytes 163856
  463.8 1.2 reshape.126
  465.8 4.8 all-to-all-start.1
  470.6 5.8 fusion.2
  476.4 215.3 %reduce-scatter.9.cloned.1.call-done = bf16[128,640]{1,0:T(8,128)(2,1)} async-done(((bf16[4096,640]{1,0:T(8,128)(2,1)}), bf16[128,640]{1,0:T(8,128)(2,1)}) %reduce-scatter.9.cloned.1.call-update) | async-done | bytes 163856
  691.7 1.2 reshape.128
  693.7 4.8 all-to-all-start.3
  698.5 2.4 fusion.13
  701.0 1.3 gather_fusion.2
  702.8 47.3 %all-gather = f32[8192,2]{0,1:T(2,128)S(1)} all-gather(f32[256,2]{0,1:T(2,128)S(1)} %bitcast.87), channel_id=2, replica_groups=mesh['section'=32,'expert'=8] {'section'}, dimensions={0}, use_global_device_ids=true | all-gather | bytes 67584 | tf_op jit(solution)/shard_map/all_gather | solution.py:76
  750.7 1.4 fusion.14
  (58 shorter events, 7.6 us)
Async XLA Ops:
  7.2 197.6 %copy-start = (bf16[1,256,4096]{2,1,0:T(8,128)(2,1)S(1)}, bf16[1,256,4096]{2,1,0:T(8,128)(2,1)}, u32[]{:S(2)}) copy-start(bf16[1,256,4096]{2,1,0:T(8,128)(2,1)} %param.12) | copy-start | bytes 6291460
  7.2 6.4 copy-start.2
  7.2 18.9 %copy-start.3 = (bf16[256,128]{1,0:T(8,128)(2,1)S(1)}, bf16[256,128]{1,0:T(8,128)(2,1)}, u32[]{:S(2)}) copy-start(bf16[256,128]{1,0:T(8,128)(2,1)} %param.13) | copy-start | bytes 196612
  7.2 108.0 %all-gather.4.cloned.1.call-start = ((), (), s32[]{:S(2)}) async-start(), calls=%async_computation.6 | async-start | bytes 5406720 | tf_op jit(solution)/shard_map/all_gather | solution.py:50
  26.0 178.7 %all-gather.6.cloned.1.call-start = ((), (), s32[]{:S(2)}) async-start(), calls=%async_computation.7 | async-start | bytes 5406720 | tf_op jit(solution)/shard_map/all_gather | solution.py:50
  37.9 425.9 %reduce-scatter.7.cloned.1.call-start = ((), (), s32[]{:S(2)}) async-start(), calls=%async_computation.8 | async-start | bytes 5406720
  115.2 5.7 copy-start.4
  115.2 5.7 copy-start.10
  238.2 1.6 copy-start.5
  238.3 453.4 %reduce-scatter.9.cloned.1.call-start = ((), (), s32[]{:S(2)}) async-start(), calls=%async_computation.9 | async-start | bytes 5406720
  239.8 2.7 copy-start.6
  239.8 2.7 copy-start.8
  270.7 1.0 copy-start.9
  271.7 5.7 copy-start.7
  465.8 227.9 %all-to-all-start.1 = ((bf16[8,80,128]{2,1,0:T(8,128)(2,1)}), bf16[8,80,128]{2,1,0:T(8,128)(2,1)S(1)}, u32[]{:S(2)}, u32[]{:S(2)}) async-start(bf16[8,80,128]{2,1,0:T(8,128)(2,1)} %copy.37), calls=%async_computation.1 | async-start | bytes 327680 | tf_op jit(solution)/shard_map/all_to_all | solution.py:60
  470.6 281.4 %copy-start.1 = (bf16[1,256,4096]{2,1,0:T(8,128)(2,1)S(1)}, bf16[1,256,4096]{2,1,0:T(8,128)(2,1)}, u32[]{:S(2)}) copy-start(bf16[1,256,4096]{2,1,0:T(8,128)(2,1)} %param.12) | copy-start | bytes 6291460
  693.7 57.0 %all-to-all-start.3 = ((bf16[8,80,128]{2,1,0:T(8,128)(2,1)}), bf16[8,80,128]{2,1,0:T(8,128)(2,1)S(1)}, u32[]{:S(2)}, u32[]{:S(2)}) async-start(bf16[8,80,128]{2,1,0:T(8,128)(2,1)} %copy.39), calls=%async_computation.3 | async-start | bytes 327680 | tf_op jit(solution)/shard_map/all_to_all | solution.py:60
Sparse Core Ops, SparseCore 0:
  26.1 88.9 all-gather.3
  117.6 87.0 all-gather.5
  238.4 225.3 reduce-scatter.6
  467.6 224.0 reduce-scatter.8
